TPU v7x, 128 devices: a whole 4x4x4 slice. The times are simulated.
128 devices in a mesh: sector: 16 (over z, x_lo, core), tm: 2 (over x_hi), space: 4 (over y).
Axes of the slice: x: 4 (x_hi: 2, x_lo: 2; x = x_hi * 2 + x_lo), y: 4, z: 4, core: 2. Of those that a mesh axis runs over, the one named last changes fastest.
Arguments:
- records: bfloat16 [16, 592, 3, 8192], P('sector', 'tm', None, 'space'), may hold values from -6 to 6
- block_start: int32 [16], replicated, may hold values from 0 to 231, as said below
- slab_index: int32 [8192], P('space'), may hold values from 0 to 15
- weight_table: float32 [16], replicated, may hold values from 0.25 to 4
Outputs:
- mode_fields: bfloat16 [8, 32, 2, 8, 3, 8192], P(None, ('sector', 'tm'), None, None, None, 'space')
- energy: float32 [8, 32, 8], P(None, ('sector', 'tm'))
Inputs may be any that keep to these rules, and one draw needn't show every extreme that they name: `block_start`: block j of each record (j < 8) starts at j * 32 plus 0 to 7 snapshots.
All inputs are finite; a program needn't handle non-finite values.
Results may differ from a plain program's by a relative error of at most 0.02.
Values may be sent and summed in bfloat16 or wider, within the bound.
A program may use at most 64 MiB of HBM per device.

v0:
```python
import math

import jax
import jax.numpy as jnp
from jax import lax
from jax.sharding import PartitionSpec as P

NFFT = 64
NFREQ = 32
MODES = 8
SUBIT = 4


EPSILON = 1e-06


def copy_for_each(array, axis):
    size = lax.axis_size(axis)
    return lax.all_to_all(
        jnp.broadcast_to(array[None], (size, *array.shape)), axis, 0, 0, tiled=True
    )


def taken_together(array, axis):
    return copy_for_each(array, axis).sum(axis=0)


def packed_total(arrays, axis):
    ends = [0]
    for a in arrays:
        ends.append(ends[-1] + a.size)
    subtotal = taken_together(jnp.concatenate([a.ravel() for a in arrays]), axis)
    return tuple((subtotal[b:e].reshape(a.shape) for a, b, e in zip(arrays, ends, ends[1:])))


def time_table(length, freq_count):
    steps_t = jnp.arange(length, dtype=jnp.float32)
    freq_f = jnp.arange(freq_count, dtype=jnp.float32)
    window = 0.5 - 0.5 * jnp.cos(2.0 * math.pi * steps_t / length)
    angles = 2.0 * math.pi * freq_f[:, None] * steps_t[None, :] / length
    both = jnp.stack([window * jnp.cos(angles), -window * jnp.sin(angles)])
    return (both / math.sqrt(length)).astype(jnp.bfloat16)


def order_table(orders, sectors):
    order_m = jnp.arange(orders, dtype=jnp.float32)[:, None]
    sector_s = jnp.arange(sectors, dtype=jnp.float32)[None, :]
    angles = 2.0 * math.pi * order_m * sector_s / sectors
    cosine = jnp.cos(angles)
    sine_part = jnp.sin(angles)
    upper_row = jnp.stack([cosine, sine_part], -1)
    lower_row = jnp.stack([-sine_part, cosine], -1)
    return (jnp.stack([upper_row, lower_row], 1) / math.sqrt(sectors)).astype(jnp.bfloat16)


def matmul_high(left_side, right_side):
    return jnp.matmul(left_side, right_side)


def subspace(gram_re, gram_im):
    order_size = gram_re.shape[-1]
    basis_re = jnp.broadcast_to(
        jnp.eye(order_size, MODES, dtype=jnp.float32), gram_re.shape[:-1] + (MODES,)
    )
    basis_im = jnp.zeros_like(basis_re)
    for sweep in range(SUBIT):
        image_re = matmul_high(gram_re, basis_re) - matmul_high(gram_im, basis_im)
        image_im = matmul_high(gram_re, basis_im) + matmul_high(gram_im, basis_re)
        done_re = []
        done_im = []
        for column in range(MODES):
            vec_re = image_re[..., column]
            vec_im = image_im[..., column]
            for earlier in range(column):
                old_re = done_re[earlier]
                old_im = done_im[earlier]
                proj_re = jnp.sum(old_re * vec_re + old_im * vec_im, -1, keepdims=True)
                proj_im = jnp.sum(old_re * vec_im - old_im * vec_re, -1, keepdims=True)
                vec_re = vec_re - (proj_re * old_re - proj_im * old_im)
                vec_im = vec_im - (proj_re * old_im + proj_im * old_re)
            length_v = jnp.sqrt(
                jnp.sum(vec_re * vec_re + vec_im * vec_im, -1, keepdims=True) + EPSILON
            )
            done_re.append(vec_re / length_v)
            done_im.append(vec_im / length_v)
        basis_re = jnp.stack(done_re, -1)
        basis_im = jnp.stack(done_im, -1)
    return (basis_re, basis_im)


def cell_weight(slab_rows, weight_table):
    choose = (
        slab_rows[:, None] == jnp.arange(weight_table.shape[0], dtype=jnp.int32)[None, :]
    ).astype(jnp.float32)
    return jnp.dot(choose, weight_table)


def gram(coeffs, weight):
    weighted = (coeffs.astype(jnp.float32) * weight).astype(jnp.bfloat16)
    products = jnp.einsum(
        "mcbfkx,mdefkx->mfcbde", weighted, coeffs, preferred_element_type=jnp.float32
    )
    gram_re = products[:, :, 0, :, 0, :] + products[:, :, 1, :, 1, :]
    gram_im = products[:, :, 0, :, 1, :] - products[:, :, 1, :, 0, :]
    return (gram_re, gram_im)


def finish(coeffs, gram_re, gram_im, weight, cell_total):
    basis_re, basis_im = subspace(gram_re, gram_im)
    image_re = matmul_high(gram_re, basis_re) - matmul_high(gram_im, basis_im)
    image_im = matmul_high(gram_re, basis_im) + matmul_high(gram_im, basis_re)
    energy = jnp.sum(basis_re * image_re + basis_im * image_im, -2) / cell_total
    short_re = basis_re.astype(jnp.bfloat16)
    short_im = basis_im.astype(jnp.bfloat16)
    first_row = jnp.stack([short_re, short_im], -2)
    second_row = jnp.stack([-short_im, short_re], -2)
    mixing = jnp.stack([first_row, second_row], 2)
    fields_out = jnp.einsum(
        "mcbfkx,mfcbdj->mfdjkx", coeffs, mixing, preferred_element_type=jnp.float32
    )
    factor = lax.rsqrt(energy)[:, :, None, :, None, None] * jnp.sqrt(weight)
    return ((fields_out * factor).astype(jnp.bfloat16), energy)


def local(records, block_start, slab_index, weight_table):
    sec_local, rec_len, fields, cell_local = records.shape
    sec_count = lax.axis_size("sector")
    tm_count = lax.axis_size("tm")
    block_count = block_start.shape[0] // tm_count
    order_total = sec_local * sec_count // 2
    time_basis = time_table(NFFT, NFREQ)
    azimuth = order_table(order_total, sec_local * sec_count)
    own_starts = lax.dynamic_slice_in_dim(
        block_start, lax.axis_index("tm") * block_count, block_count
    )

    def spectra_of(start_at):
        segment = lax.dynamic_slice_in_dim(records, start_at, NFFT, 1)
        return jnp.einsum(
            "cft,stkx->scfkx", time_basis, segment, preferred_element_type=jnp.float32
        ).astype(jnp.bfloat16)

    spectra = lax.map(spectra_of, own_starts)
    arrived = lax.all_to_all(
        spectra[None], ("sector", "tm"), split_axis=4, concat_axis=0, tiled=True
    )
    arrived = arrived.reshape((sec_count, tm_count) + arrived.shape[1:])
    coeffs = jnp.einsum(
        "mcase,ajbsefkx->mcjbfkx",
        azimuth.reshape(order_total, 2, sec_count, sec_local, 2),
        arrived,
        preferred_element_type=jnp.float32,
    ).astype(jnp.bfloat16)
    coeffs = coeffs.reshape((order_total, 2, tm_count * block_count) + coeffs.shape[4:])
    weight = cell_weight(slab_index, weight_table)
    gram_re, gram_im = gram(coeffs, weight)
    gram_re, gram_im = packed_total((gram_re, gram_im), "space")
    cell_total = fields * cell_local * lax.axis_size("space")
    mode_fields, energy = finish(coeffs, gram_re, gram_im, weight, cell_total)
    return (mode_fields, energy)


def solution(mesh):
    placed = (P("sector", "tm", None, "space"), P(), P("space"), P())
    return jax.shard_map(
        local,
        mesh=mesh,
        in_specs=placed,
        out_specs=(
            P(None, ("sector", "tm"), None, None, None, "space"),
            P(None, ("sector", "tm"), None),
        ),
        check_vma=False,
    )
```

profile of v0, /device:TPU:1, one launch (start us, length us, event | category | flops | bytes accessed | tf_op | source)
XLA Modules:
  0.0 201.6 jit_solution(16157958276227727423)
XLA Ops:
  0.9 0.7 dynamic_slice.10
  1.6 39.9 %while.10 = (s32[]{:T(128)}, bf16[8,1,2,32,3,2048]{5,3,2,4,1,0:T(8,128)(2,1)}, s32[8]{0:T(128)S(1)}, bf16[1,296,3,2048]{3,1,2,0:T(8,128)(2,1)}, bf16[2,32,64]{2,...) while((s32[]{:T(128)}, bf16[8,1,2,32,3,2048]{5,3,2,4,1,0:T(8,128)(2,1)}, s32[8]{0:T(128)S(1)}, ...), condition=%wide.region_1.2_spmd, body=%wide.region_0.1_spmd.sunk | while | flops 50724868 | bytes 1581703 | solution.py:143
  1.6 0.6 dynamic_slice.18
  4.2 2.4 %fusion.258 = bf16[8,1,2,32,3,2048]{5,3,2,4,1,0:T(8,128)(2,1)} fusion(bf16[8,1,2,32,3,2048]{5,3,2,4,1,0:T(8,128)(2,1)} %get-tuple-element.776, s32[]{:T(128)} %get-tuple-element.775, bf16[1,296,3,2048]{3,1,2,0:T(8,128)(2,1)} %get-tuple-element.786, s32[]{:T(128)S(6)} %select_n.8, bf16[2,32,64]{2,1,0:T(8,128)(2,1)S(1)} %get-tuple-element.787), kind=kOutput, calls=%fused_computation.2.clone.1 | convolution fusion | flops 50724864 | bytes 1581572 | tf_op jit(solution)/shard_map/while/body/eval_jaxpr/cft,stkx->scfkx/dot_general | solution.py:139
  6.6 0.6 dynamic_slice.18
  9.1 2.4 %fusion.258 = bf16[8,1,2,32,3,2048]{5,3,2,4,1,0:T(8,128)(2,1)} fusion(bf16[8,1,2,32,3,2048]{5,3,2,4,1,0:T(8,128)(2,1)} %get-tuple-element.776, s32[]{:T(128)} %get-tuple-element.775, bf16[1,296,3,2048]{3,1,2,0:T(8,128)(2,1)} %get-tuple-element.786, s32[]{:T(128)S(6)} %select_n.8, bf16[2,32,64]{2,1,0:T(8,128)(2,1)S(1)} %get-tuple-element.787), kind=kOutput, calls=%fused_computation.2.clone.1 | convolution fusion | flops 50724864 | bytes 1581572 | tf_op jit(solution)/shard_map/while/body/eval_jaxpr/cft,stkx->scfkx/dot_general | solution.py:139
  11.6 0.6 dynamic_slice.18
  14.1 2.5 %fusion.258 = bf16[8,1,2,32,3,2048]{5,3,2,4,1,0:T(8,128)(2,1)} fusion(bf16[8,1,2,32,3,2048]{5,3,2,4,1,0:T(8,128)(2,1)} %get-tuple-element.776, s32[]{:T(128)} %get-tuple-element.775, bf16[1,296,3,2048]{3,1,2,0:T(8,128)(2,1)} %get-tuple-element.786, s32[]{:T(128)S(6)} %select_n.8, bf16[2,32,64]{2,1,0:T(8,128)(2,1)S(1)} %get-tuple-element.787), kind=kOutput, calls=%fused_computation.2.clone.1 | convolution fusion | flops 50724864 | bytes 1581572 | tf_op jit(solution)/shard_map/while/body/eval_jaxpr/cft,stkx->scfkx/dot_general | solution.py:139
  16.6 0.6 dynamic_slice.18
  19.1 2.5 %fusion.258 = bf16[8,1,2,32,3,2048]{5,3,2,4,1,0:T(8,128)(2,1)} fusion(bf16[8,1,2,32,3,2048]{5,3,2,4,1,0:T(8,128)(2,1)} %get-tuple-element.776, s32[]{:T(128)} %get-tuple-element.775, bf16[1,296,3,2048]{3,1,2,0:T(8,128)(2,1)} %get-tuple-element.786, s32[]{:T(128)S(6)} %select_n.8, bf16[2,32,64]{2,1,0:T(8,128)(2,1)S(1)} %get-tuple-element.787), kind=kOutput, calls=%fused_computation.2.clone.1 | convolution fusion | flops 50724864 | bytes 1581572 | tf_op jit(solution)/shard_map/while/body/eval_jaxpr/cft,stkx->scfkx/dot_general | solution.py:139
  21.6 0.6 dynamic_slice.18
  24.2 2.4 %fusion.258 = bf16[8,1,2,32,3,2048]{5,3,2,4,1,0:T(8,128)(2,1)} fusion(bf16[8,1,2,32,3,2048]{5,3,2,4,1,0:T(8,128)(2,1)} %get-tuple-element.776, s32[]{:T(128)} %get-tuple-element.775, bf16[1,296,3,2048]{3,1,2,0:T(8,128)(2,1)} %get-tuple-element.786, s32[]{:T(128)S(6)} %select_n.8, bf16[2,32,64]{2,1,0:T(8,128)(2,1)S(1)} %get-tuple-element.787), kind=kOutput, calls=%fused_computation.2.clone.1 | convolution fusion | flops 50724864 | bytes 1581572 | tf_op jit(solution)/shard_map/while/body/eval_jaxpr/cft,stkx->scfkx/dot_general | solution.py:139
  26.6 0.6 dynamic_slice.18
  29.1 2.5 %fusion.258 = bf16[8,1,2,32,3,2048]{5,3,2,4,1,0:T(8,128)(2,1)} fusion(bf16[8,1,2,32,3,2048]{5,3,2,4,1,0:T(8,128)(2,1)} %get-tuple-element.776, s32[]{:T(128)} %get-tuple-element.775, bf16[1,296,3,2048]{3,1,2,0:T(8,128)(2,1)} %get-tuple-element.786, s32[]{:T(128)S(6)} %select_n.8, bf16[2,32,64]{2,1,0:T(8,128)(2,1)S(1)} %get-tuple-element.787), kind=kOutput, calls=%fused_computation.2.clone.1 | convolution fusion | flops 50724864 | bytes 1581572 | tf_op jit(solution)/shard_map/while/body/eval_jaxpr/cft,stkx->scfkx/dot_general | solution.py:139
  31.6 0.6 dynamic_slice.18
  34.1 2.5 %fusion.258 = bf16[8,1,2,32,3,2048]{5,3,2,4,1,0:T(8,128)(2,1)} fusion(bf16[8,1,2,32,3,2048]{5,3,2,4,1,0:T(8,128)(2,1)} %get-tuple-element.776, s32[]{:T(128)} %get-tuple-element.775, bf16[1,296,3,2048]{3,1,2,0:T(8,128)(2,1)} %get-tuple-element.786, s32[]{:T(128)S(6)} %select_n.8, bf16[2,32,64]{2,1,0:T(8,128)(2,1)S(1)} %get-tuple-element.787), kind=kOutput, calls=%fused_computation.2.clone.1 | convolution fusion | flops 50724864 | bytes 1581572 | tf_op jit(solution)/shard_map/while/body/eval_jaxpr/cft,stkx->scfkx/dot_general | solution.py:139
  36.6 0.6 dynamic_slice.18
  39.1 2.4 %fusion.258 = bf16[8,1,2,32,3,2048]{5,3,2,4,1,0:T(8,128)(2,1)} fusion(bf16[8,1,2,32,3,2048]{5,3,2,4,1,0:T(8,128)(2,1)} %get-tuple-element.776, s32[]{:T(128)} %get-tuple-element.775, bf16[1,296,3,2048]{3,1,2,0:T(8,128)(2,1)} %get-tuple-element.786, s32[]{:T(128)S(6)} %select_n.8, bf16[2,32,64]{2,1,0:T(8,128)(2,1)S(1)} %get-tuple-element.787), kind=kOutput, calls=%fused_computation.2.clone.1 | convolution fusion | flops 50724864 | bytes 1581572 | tf_op jit(solution)/shard_map/while/body/eval_jaxpr/cft,stkx->scfkx/dot_general | solution.py:139
  41.6 8.9 %copy.381 = bf16[8,1,2,32,3,2048]{5,0,4,2,3,1:T(8,128)(2,1)} copy(bf16[8,1,2,32,3,2048]{5,3,2,4,1,0:T(8,128)(2,1)} %get-tuple-element.29) | data formatting | bytes 12582912 | tf_op jit(solution)/shard_map/while | solution.py:143
  50.5 9.6 %all-to-all-start = ((bf16[1,8,1,2,32,3,2048]{6,1,5,3,2,0,4:T(8,128)(2,1)}), bf16[1,8,1,2,32,3,2048]{6,1,5,3,2,0,4:T(8,128)(2,1)}, u32[]{:S(2)}, u32[]{:S(2)}) async-start(bf16[1,8,1,2,32,3,2048]{6,1,5,3,2,0,4:T(8,128)(2,1)} %bitcast.909), calls=%async_computation | async-start | bytes 12582912 | tf_op jit(solution)/shard_map/all_to_all | solution.py:144
  60.2 0.5 fusion.34
  60.7 85.5 %all-to-all-done = bf16[1,8,1,2,32,3,2048]{6,1,5,3,2,0,4:T(8,128)(2,1)} async-done(((bf16[1,8,1,2,32,3,2048]{6,1,5,3,2,0,4:T(8,128)(2,1)}), bf16[1,8,1,2,32,3,2048]{6,1,5,3,2,0,4:T(8,128)(2,1)}, u32[]{:S(2)}, u32[]{:S(2)}) %all-to-all-start) | async-done | bytes 6291488 | tf_op jit(solution)/shard_map/all_to_all | solution.py:144
  146.2 9.6 %bitcast_convert_fusion = bf16[8,2,2,8,3,2048]{5,0,4,3,2,1:T(8,128)(2,1)S(1)} fusion(bf16[16,2,8,2,3,2048]{5,2,4,3,1,0:T(8,128)(2,1)} %bitcast.15, f32[8,1,16,2]{2,0,3,1:T(8,128)S(1)} %get-tuple-element.728, f32[8,1,16,2]{2,0,3,1:T(8,128)S(1)} %get-tuple-element.727), kind=kOutput, calls=%fused_computation.7 | convolution fusion | flops 102237696 | bytes 9439232 | tf_op jit(solution)/shard_map/mcase,ajbsefkx->mcjbfkx/dot_general | solution.py:148
  155.8 4.9 %fusion.25 = f32[8,1,2,16,2,16]{5,3,4,2,0,1:T(8,128)S(1)} fusion(bf16[8,2,16,3,2048,1]{4,0,3,2,1,5:T(8,128)(2,1)S(1)} %bitcast.910, bf16[8,2,16,3,2048]{4,0,3,2,1:T(8,128)(2,1)S(1)} %bitcast.911, f32[2048]{0:T(1024)S(1)} %bitcast.945), kind=kOutput, calls=%fused_computation.23 | convolution fusion | flops 105381888 | bytes 6332416 | tf_op jit(solution)/shard_map/mcbfkx,mdefkx->mfcbde/dot_general | solution.py:100
  160.9 0.7 broadcast_in_dim.12
  161.6 4.2 %all-to-all-start.1 = ((f32[4,1,4096]{2,1,0:T(1,128)}), f32[4,1,4096]{2,1,0:T(1,128)S(1)}, u32[]{:S(2)}, u32[]{:S(2)}) async-start(f32[4,1,4096]{2,1,0:T(1,128)} %broadcast_in_dim.12), calls=%async_computation.1 | async-start | bytes 131072 | tf_op jit(solution)/shard_map/all_to_all | solution.py:19
  165.8 4.5 %all-to-all-done.1 = f32[4,1,4096]{2,1,0:T(1,128)S(1)} async-done(((f32[4,1,4096]{2,1,0:T(1,128)}), f32[4,1,4096]{2,1,0:T(1,128)S(1)}, u32[]{:S(2)}, u32[]{:S(2)}) %all-to-all-start.1) | async-done | bytes 65568 | tf_op jit(solution)/shard_map/all_to_all | solution.py:19
  171.2 0.3 fusion.180
  172.0 0.4 add_reduce_fusion.90
  172.6 0.4 add_reduce_fusion.89
  173.2 0.3 add_reduce_fusion.88
  173.7 0.3 add_reduce_fusion.87
  174.2 0.2 add_reduce_fusion.86
  174.6 0.2 add_reduce_fusion.85
  175.7 0.2 constant_dynamic-update-slice_fusion.8
  176.8 0.2 constant_dynamic-update-slice_fusion
  177.4 0.3 fusion.150
  178.2 0.4 add_reduce_fusion.62
  178.8 0.4 add_reduce_fusion.61
  179.4 0.3 add_reduce_fusion.60
  179.9 0.3 add_reduce_fusion.59
  180.4 0.2 add_reduce_fusion.58
  180.8 0.2 add_reduce_fusion.57
  182.0 0.2 constant_dynamic-update-slice_fusion.24
  183.0 0.2 constant_dynamic-update-slice_fusion.16
  183.6 0.3 fusion.120
  184.4 0.4 add_reduce_fusion.34
  185.0 0.4 add_reduce_fusion.33
  185.6 0.3 add_reduce_fusion.32
  186.1 0.3 add_reduce_fusion.31
  186.6 0.2 add_reduce_fusion.30
  187.0 0.2 add_reduce_fusion.29
  188.3 0.2 constant_dynamic-update-slice_fusion.40
  189.2 0.2 constant_dynamic-update-slice_fusion.32
  189.8 0.3 fusion.90
  190.6 0.4 add_reduce_fusion.6
  191.2 0.4 add_reduce_fusion.5
  191.7 0.3 add_reduce_fusion.4
  192.2 0.3 add_reduce_fusion.3
  192.7 0.2 add_reduce_fusion.2
  193.2 0.2 add_reduce_fusion.1
  195.6 0.2 fusion.33
  195.8 0.6 broadcast_multiply_fusion.1
  196.6 5.0 %fusion.22 = bf16[8,1,2,8,3,2048]{5,3,4,2,1,0:T(8,128)(2,1)} fusion(bf16[8,2,16,3,2048,1]{4,0,3,2,1,5:T(8,128)(2,1)S(1)} %bitcast.912, f32[8,8,2048]{2,1,0:T(8,128)S(1)} %broadcast_multiply_fusion, bf16[8,1,1,16,2,8]{3,5,2,4,0,1:T(8,128)(2,1)S(1)} %get-tuple-element.706, bf16[8,1,1,16,2,8]{3,5,2,4,0,1:T(8,128)(2,1)S(1)} %get-tuple-element.705), kind=kOutput, calls=%fused_computation.22 | convolution fusion | flops 51920896 | bytes 5251072 | tf_op jit(solution)/shard_map/mcbfkx,mfcbdj->mfdjkx/dot_general | solution.py:118
  (199 shorter events, 15.8 us)
Async XLA Ops:
  0.6 59.6 %copy-start = (f32[16]{0:T(128)S(1)}, f32[16]{0:T(128)}, u32[]{:S(2)}) copy-start(f32[16]{0:T(128)} %param.9) | copy-start | bytes 196
  50.4 9.8 %copy-start.1 = (s32[2048]{0:T(1024)S(1)}, s32[2048]{0:T(1024)}, u32[]{:S(2)}) copy-start(s32[2048]{0:T(1024)} %param.8) | copy-start | bytes 24580
  50.5 95.7 %all-to-all-start = ((bf16[1,8,1,2,32,3,2048]{6,1,5,3,2,0,4:T(8,128)(2,1)}), bf16[1,8,1,2,32,3,2048]{6,1,5,3,2,0,4:T(8,128)(2,1)}, u32[]{:S(2)}, u32[]{:S(2)}) async-start(bf16[1,8,1,2,32,3,2048]{6,1,5,3,2,0,4:T(8,128)(2,1)} %bitcast.909), calls=%async_computation | async-start | bytes 12582912 | tf_op jit(solution)/shard_map/all_to_all | solution.py:144
  161.6 8.7 %all-to-all-start.1 = ((f32[4,1,4096]{2,1,0:T(1,128)}), f32[4,1,4096]{2,1,0:T(1,128)S(1)}, u32[]{:S(2)}, u32[]{:S(2)}) async-start(f32[4,1,4096]{2,1,0:T(1,128)} %broadcast_in_dim.12), calls=%async_computation.1 | async-start | bytes 131072 | tf_op jit(solution)/shard_map/all_to_all | solution.py:19
where the time goes:
time: 204 us; the launch traced here: 202 us
  waiting for transfers between devices  90 us (44%)
  matrix products  42.3 us (21%)
  other arithmetic  22.9 us (11%)
  local copies, waits for them, and re-layouts  15.8 us (8%)
  loops' own time  15.6 us (8%)
  starting transfers between devices  13.8 us (7%)
    all_to_all x1, waiting for transfers between devices, local(): lax.all_to_all(spectra[None], ('sector', 'tm'), split_axis=4, concat_axis...  85.5 us
    dot_general x8, matrix products, spectra_of(): jnp.einsum('cft,stkx->scfkx', time_basis, segment, preferred_element_type...  19.7 us
    another operation x1, loops' own time, local(): spectra = lax.map(spectra_of, own_starts)  15.6 us
    dot_general x1, matrix products, local(): jnp.einsum('mcase,ajbsefkx->mcjbfkx', azimuth.reshape(order_total, 2, sec...  9.64 us
    all_to_all x1, starting transfers between devices, local(): lax.all_to_all(spectra[None], ('sector', 'tm'), split_axis=4, concat_axis...  9.61 us
    reduce_sum x32, other arithmetic, subspace(): proj_re = jnp.sum(old_re * vec_re + old_im * vec_im, -1, keepdims=True)  9.13 us
    while x1, local copies, waits for them, and re-layouts, local(): spectra = lax.map(spectra_of, own_starts)  8.89 us
    reduce_sum x32, other arithmetic, subspace(): jnp.sum(vec_re * vec_re + vec_im * vec_im, -1, keepdims=True) + EPSILON  5.8 us
  transfers between devices with their start and end apart: 2, of which 2 were waited for; matrix products, arithmetic and copies ran while one was open for 0% of the time, Pallas kernels for 0%

commit v1 on v0

v1 whole, which is shorter than its diff:
```python
import functools

import jax
import jax.numpy as jnp
import ml_dtypes
import numpy as np
from jax import lax
from jax.experimental import pallas as pl
from jax.experimental.pallas import tpu as pltpu
from jax.sharding import PartitionSpec as P

NFFT = 64
NFREQ = 32
MODES = 8
SUBIT = 4
EPSILON = 1e-06
MESH = pl.DeviceIdType.MESH
BF = jnp.bfloat16
F32 = jnp.float32

SECTORS = 16
ORDERS = 8
TMS = 2
SPACE = 4
BLK = 8
BLOCKS = TMS * BLK
FIELDS = 3
TREC = 296
CELLS = 2048
NSLAB = 16
SLOTS = TMS * SECTORS
ROWS = 2 * BLK
LANES = 128
TILE = 512


def time_table():
    t = np.arange(NFFT, dtype=np.float32)
    f = np.arange(NFREQ, dtype=np.float32)
    two_pi = np.float32(2.0 * np.pi)
    window = np.float32(0.5) - np.float32(0.5) * np.cos(two_pi * t / np.float32(NFFT))
    angles = two_pi * f[:, None] * t[None, :] / np.float32(NFFT)
    both = np.stack([window * np.cos(angles), -window * np.sin(angles)])
    return (both / np.float32(np.sqrt(NFFT))).astype(ml_dtypes.bfloat16)


def order_table():
    m = np.arange(ORDERS, dtype=np.float32)[:, None]
    s = np.arange(SECTORS, dtype=np.float32)[None, :]
    angles = np.float32(2.0 * np.pi) * m * s / np.float32(SECTORS)
    cosine, sine = np.cos(angles), np.sin(angles)
    both = np.stack([np.stack([cosine, sine], -1), np.stack([-sine, cosine], -1)], 1)
    return (both / np.float32(np.sqrt(SECTORS))).astype(ml_dtypes.bfloat16)


def spread_time_table():
    basis = time_table().astype(np.float32)
    wide = np.zeros((NFREQ, BLK, 2, BLK, NFFT), np.float32)
    for b in range(BLK):
        wide[:, b, :, b, :] = basis.transpose(1, 0, 2)
    return wide.reshape(NFREQ * ROWS, BLK * NFFT).astype(ml_dtypes.bfloat16)


def spread_order_table():
    table = order_table().astype(np.float32)
    wide = np.zeros((2, ORDERS, TMS, BLK, TMS, SECTORS, BLK, 2), np.float32)
    for j in range(TMS):
        for b in range(BLK):
            wide[:, :, j, b, j, :, b, :] = table.transpose(1, 0, 2, 3)
    return wide.reshape(2 * ORDERS * BLOCKS, SLOTS * ROWS).astype(ml_dtypes.bfloat16)


def place():
    sector, tm, y = lax.axis_index("sector"), lax.axis_index("tm"), lax.axis_index("space")
    return tm * 2 + (sector // 2) % 2, y, sector // 4, sector % 2


def device_at(x, y, z, core):
    return (z * 4 + (x % 2) * 2 + core, x // 2, y)


def send_order():
    dist = (0, 1, 2, 1)
    offsets = [
        (a, b, c) for a in range(4) for b in range(4) for c in range(2) if (a, b, c) != (0, 0, 0)
    ]
    offsets.sort(key=lambda o: -(dist[o[0]] + dist[o[1]]))
    order = []
    for a, b, c in offsets:
        for o in ((a, b, c), (-a % 4, -b % 4, c), (b, a, c), (-b % 4, -a % 4, c)):
            if o not in order:
                order.append(o)
    return order


ORDER = send_order()


def weight_row(slab_ref, table_ref):
    slab = slab_ref[...]
    weight = jnp.zeros(slab.shape, F32)
    for n in range(NSLAB):
        weight = jnp.where(slab == n, table_ref[n], weight)
    return weight


def gather_kernel(
    rec_hbm, start_ref, table_ref, slab_ref, basis_ref, order_ref, coef_hbm, gram_ref,
    rec, send, recv, coef, band, shift, weight, acc, slots,
    rec_sem, own_sem, send_sem, recv_sem, coef_sem, gsend_sem, grecv_sem,
):
    x, y, z, core = place()
    tm = x // 2
    own = tm * SECTORS + z * 4 + (x % 2) * 2 + core

    def peer(offset):
        a, b, c = offset
        return (x + a + core * (b - a)) % 4, y, (z + b + core * (a - b)) % 4, (core + c) % 2

    barrier = pltpu.get_barrier_semaphore()
    for offset in ORDER:
        pl.semaphore_signal(barrier, inc=1, device_id=device_at(*peer(offset)), device_id_type=MESH)
    for d in range(1, SPACE):
        pl.semaphore_signal(
            barrier, inc=1, device_id=device_at(x, (y + d) % SPACE, z, core), device_id_type=MESH
        )
    loads = [
        pltpu.make_async_copy(rec_hbm.at[k], rec.at[k], rec_sem.at[k]) for k in range(FIELDS)
    ]
    for load in loads:
        load.start()

    weight[...] = weight_row(slab_ref, table_ref)
    step = lax.broadcasted_iota(jnp.int32, (NFFT, TREC), 1) - lax.broadcasted_iota(
        jnp.int32, (NFFT, TREC), 0
    )
    for b in range(BLK):
        shift[b * NFFT : (b + 1) * NFFT, :] = jnp.where(
            step == start_ref[tm * BLK + b], 1.0, 0.0
        ).astype(BF)
    band[...] = jnp.dot(basis_ref[...], shift[...], preferred_element_type=F32).astype(BF)

    copies, owns = [], []
    for k in range(FIELDS):
        loads[k].wait()

        @pl.loop(0, CELLS // TILE)
        def _(t):
            cols = pl.ds(pl.multiple_of(t * TILE, TILE), TILE)
            out = jnp.dot(band[...], rec[k, :, cols], preferred_element_type=F32)
            send[k, :, :, cols] = out.astype(BF).reshape(NFREQ, ROWS, TILE)

        if k == 0:
            pl.semaphore_wait(barrier, len(ORDER) + SPACE - 1)
        for i, offset in enumerate(ORDER):
            px, py, pz, pc = peer(offset)
            sector, ptm, _ = device_at(px, py, pz, pc)
            copy = pltpu.make_async_remote_copy(
                src_ref=send.at[k, sector * TMS + ptm],
                dst_ref=recv.at[k, own],
                send_sem=send_sem.at[k, i],
                recv_sem=recv_sem.at[k, i],
                device_id=device_at(px, py, pz, pc),
                device_id_type=MESH,
            )
            copy.start()
            copies.append(copy)
        sector, ptm, _ = device_at(x, y, z, core)
        mine = pltpu.make_async_copy(
            send.at[k, sector * TMS + ptm], recv.at[k, own], own_sem.at[k]
        )
        mine.start()
        owns.append(mine)

    acc[...] = jnp.zeros_like(acc)
    stores = []
    for k in range(FIELDS):
        for copy in copies[k * len(ORDER) : (k + 1) * len(ORDER)]:
            copy.wait_recv()
        owns[k].wait()

        @pl.loop(0, CELLS // TILE)
        def _(t):
            cols = pl.ds(pl.multiple_of(t * TILE, TILE), TILE)
            arrived = recv[k, :, :, cols].reshape(SLOTS * ROWS, TILE)
            c = jnp.dot(order_ref[...], arrived, preferred_element_type=F32).astype(BF)
            coef[k, :, cols] = c
            weighted = (c.astype(F32) * weight[:, cols]).astype(BF)
            acc[...] += lax.dot_general(
                weighted, c, (((1,), (1,)), ((), ())), preferred_element_type=F32
            )

        store = pltpu.make_async_copy(coef.at[k], coef_hbm.at[k], coef_sem.at[k])
        store.start()
        stores.append(store)

    half = ORDERS * BLOCKS
    full_re = acc[:half, :half] + acc[half:, half:]
    full_im = acc[:half, half:] - acc[half:, :half]
    group = lax.broadcasted_iota(jnp.int32, (BLOCKS, half), 1) // BLOCKS
    gram_re = jnp.zeros((BLOCKS, half), F32)
    gram_im = jnp.zeros((BLOCKS, half), F32)
    for m in range(ORDERS):
        rows = slice(m * BLOCKS, (m + 1) * BLOCKS)
        gram_re = jnp.where(group == m, full_re[rows], gram_re)
        gram_im = jnp.where(group == m, full_im[rows], gram_im)
    slots[y, 0] = gram_re
    slots[y, 1] = gram_im
    swaps = []
    for d in range(1, SPACE):
        swap = pltpu.make_async_remote_copy(
            src_ref=slots.at[y],
            dst_ref=slots.at[y],
            send_sem=gsend_sem.at[d - 1],
            recv_sem=grecv_sem.at[d - 1],
            device_id=device_at(x, (y + d) % SPACE, z, core),
            device_id_type=MESH,
        )
        swap.start()
        swaps.append(swap)
    for swap in swaps:
        swap.wait_recv()
    gram_ref[...] = (slots[0] + slots[1]) + (slots[2] + slots[3])
    for swap in swaps:
        swap.wait_send()
    for copy in copies:
        copy.wait_send()
    for store in stores:
        store.wait()


def take(array, index):
    return jnp.take_along_axis(array, index, axis=1)


def modes_kernel(
    coef_hbm, gram_ref, table_ref, slab_ref, out_hbm, energy_ref,
    coef, out, mix, scale, root, coef_sem, out_sem,
):
    loads = [
        pltpu.make_async_copy(coef_hbm.at[k], coef.at[k], coef_sem.at[k]) for k in range(FIELDS)
    ]
    for load in loads:
        load.start()
    root[...] = jnp.sqrt(weight_row(slab_ref, table_ref))

    shape = (BLOCKS, LANES)
    lane = lax.broadcasted_iota(jnp.int32, shape, 1)
    low = lane < LANES // 2
    column = (lane // ORDERS) % MODES
    order = lane % ORDERS
    gram_re, gram_im = gram_ref[0], gram_ref[1]
    both = jnp.concatenate([gram_re, gram_im], 0)
    wide = (BLOCKS * ORDERS, LANES)
    same = (
        lax.broadcasted_iota(jnp.int32, wide, 0) // BLOCKS
        == lax.broadcasted_iota(jnp.int32, wide, 1) % ORDERS
    )

    def apply(re, im):
        right = jnp.where(same, jnp.concatenate([jnp.where(low, re, im)] * ORDERS, 0), 0.0)
        image = jnp.dot(
            both, right, preferred_element_type=F32, precision=lax.Precision.HIGHEST
        )
        turned = pltpu.roll(image, LANES // 2, 1)
        p0, p1, t0, t1 = image[:BLOCKS], image[BLOCKS:], turned[:BLOCKS], turned[BLOCKS:]
        return jnp.where(low, p0 - t1, t0 - p1), jnp.where(low, t0 + p1, p0 + t1)

    def total(a):
        return jnp.sum(a, axis=0, keepdims=True)

    first = order * BLOCKS + column
    re, im = take(gram_re, first), take(gram_im, first)
    for sweep in range(SUBIT):
        if sweep:
            re, im = apply(re, im)
        for i in range(MODES):
            index = order + i * ORDERS
            v_re, v_im = take(re, index), take(im, index)
            size = total(v_re * v_re + v_im * v_im) + EPSILON
            q_re = total(v_re * re + v_im * im) / size
            q_im = total(v_re * im - v_im * re) / size
            norm = lax.rsqrt(size)
            later, here = column > i, column == i
            re, im = (
                jnp.where(
                    later, re - (q_re * v_re - q_im * v_im), jnp.where(here, v_re * norm, re)
                ),
                jnp.where(
                    later, im - (q_re * v_im + q_im * v_re), jnp.where(here, v_im * norm, im)
                ),
            )
    image_re, image_im = apply(re, im)
    energy = total(re * image_re + im * image_im) * (1.0 / (FIELDS * CELLS * SPACE))
    energy = jnp.broadcast_to(energy, shape)

    sub = lax.broadcasted_iota(jnp.int32, (ORDERS, LANES), 0)
    lane8 = lax.broadcasted_iota(jnp.int32, (ORDERS, LANES), 1)
    table = take(energy[:ORDERS], (lane8 % MODES) * ORDERS + sub)
    energy_ref[:, 0, :] = table[:, :MODES]

    target = (lane % MODES) * ORDERS + lane // BLOCKS
    real = (lane // MODES) % 2 == 0
    out_re, out_im = take(re, target), take(im, target)
    diagonal = (
        lax.broadcasted_iota(jnp.int32, wide, 0) // BLOCKS
        == lax.broadcasted_iota(jnp.int32, wide, 1) // BLOCKS
    )
    upper = jnp.where(real, out_re, out_im)
    lower = jnp.where(real, -out_im, out_re)
    for c, part in enumerate((upper, lower)):
        block = jnp.where(diagonal, jnp.concatenate([part] * ORDERS, 0), 0.0)
        mix[:, c * LANES : (c + 1) * LANES] = block.T.astype(BF)
    factor = jnp.broadcast_to(lax.rsqrt(take(energy, target))[:1], (LANES, LANES)).T
    for n in range(TILE // LANES):
        scale[:, n * LANES : (n + 1) * LANES] = factor

    stores = []
    for k in range(FIELDS):
        loads[k].wait()

        @pl.loop(0, CELLS // TILE)
        def _(t):
            cols = pl.ds(pl.multiple_of(t * TILE, TILE), TILE)
            fields = jnp.dot(mix[...], coef[k, :, cols], preferred_element_type=F32)
            fields = fields * (scale[...] * root[:, cols])
            out[:, k, :, cols] = fields.astype(BF).reshape(2 * ORDERS, MODES, TILE)

        store = pltpu.make_async_copy(out.at[:, k], out_hbm.at[:, k], out_sem.at[k])
        store.start()
        stores.append(store)
    for store in stores:
        store.wait()


def local(records, block_start, slab_index, weight_table):
    assert records.shape == (1, TREC, FIELDS, CELLS)
    rec = jnp.transpose(records[0], (1, 0, 2))
    slab = slab_index.reshape(1, CELLS)
    any_spec = pl.BlockSpec(memory_space=pl.ANY)
    smem = pl.BlockSpec(memory_space=pltpu.SMEM)
    vmem = pl.BlockSpec(memory_space=pltpu.VMEM)
    dma = pltpu.SemaphoreType.DMA
    width = 2 * ORDERS * BLOCKS
    count = len(ORDER)
    coef, gram = pl.pallas_call(
        gather_kernel,
        name="gather",
        out_shape=(
            jax.ShapeDtypeStruct((FIELDS, width, CELLS), BF),
            jax.ShapeDtypeStruct((2, BLOCKS, LANES), F32),
        ),
        in_specs=[any_spec, smem, smem, vmem, vmem, vmem],
        out_specs=(any_spec, vmem),
        scratch_shapes=[
            pltpu.VMEM((FIELDS, TREC, CELLS), BF),
            pltpu.VMEM((FIELDS, NFREQ, ROWS, CELLS), BF),
            pltpu.VMEM((FIELDS, SLOTS, ROWS, CELLS), BF),
            pltpu.VMEM((FIELDS, width, CELLS), BF),
            pltpu.VMEM((NFREQ * ROWS, TREC), BF),
            pltpu.VMEM((BLK * NFFT, TREC), BF),
            pltpu.VMEM((1, CELLS), F32),
            pltpu.VMEM((width, width), F32),
            pltpu.VMEM((SPACE, 2, BLOCKS, LANES), F32),
            dma((FIELDS,)),
            dma((FIELDS,)),
            dma((FIELDS, count)),
            dma((FIELDS, count)),
            dma((FIELDS,)),
            dma((SPACE - 1,)),
            dma((SPACE - 1,)),
        ],
        compiler_params=pltpu.CompilerParams(
            collective_id=0, has_side_effects=True, vmem_limit_bytes=48 << 20
        ),
    )(rec, block_start, weight_table, slab, jnp.asarray(spread_time_table()), jnp.asarray(spread_order_table()))
    out, energy = pl.pallas_call(
        modes_kernel,
        name="modes",
        out_shape=(
            jax.ShapeDtypeStruct((2 * ORDERS, FIELDS, MODES, CELLS), BF),
            jax.ShapeDtypeStruct((ORDERS, 1, MODES), F32),
        ),
        in_specs=[any_spec, vmem, smem, vmem],
        out_specs=(any_spec, vmem),
        scratch_shapes=[
            pltpu.VMEM((FIELDS, width, CELLS), BF),
            pltpu.VMEM((2 * ORDERS, FIELDS, MODES, CELLS), BF),
            pltpu.VMEM((LANES, width), BF),
            pltpu.VMEM((LANES, TILE), F32),
            pltpu.VMEM((1, CELLS), F32),
            dma((FIELDS,)),
            dma((FIELDS,)),
        ],
        compiler_params=pltpu.CompilerParams(vmem_limit_bytes=32 << 20),
    )(coef, gram, weight_table, slab)
    out = out.reshape(ORDERS, 1, 2, FIELDS, MODES, CELLS)
    return jnp.transpose(out, (0, 1, 2, 4, 3, 5)), energy


def solution(mesh):
    assert dict(mesh.shape) == {"sector": SECTORS, "tm": TMS, "space": SPACE}
    placed = (P("sector", "tm", None, "space"), P(), P("space"), P())
    return jax.shard_map(
        local,
        mesh=mesh,
        in_specs=placed,
        out_specs=(
            P(None, ("sector", "tm"), None, None, None, "space"),
            P(None, ("sector", "tm"), None),
        ),
        check_vma=False,
    )
```

time: 204 us -> 100 us (0.49); the launches traced: 202 us -> 99.8 us
  Pallas kernels: 0 us -> 95.2 us
  waiting for transfers between devices: 90 us -> 0 us
  matrix products: 42.3 us -> 0 us
  other arithmetic: 22.9 us -> 0 us
  loops' own time: 15.6 us -> 0 us
  starting transfers between devices: 13.8 us -> 0 us
  local copies, waits for them, and re-layouts: 15.8 us -> 3.99 us
    pallas_call x0 -> x2, Pallas kernels: none -> 95.2 us  [the longest x1 86.3 us: local(): pl.pallas_call(gather_kernel, name='gather', out_shape=(jax.ShapeDtypeStr...]
    all_to_all x2 -> x0, waiting for transfers between devices: 90 us -> none  [the longest x1 85.5 us: local(): lax.all_to_all(spectra[None], ('sector', 'tm'), split_axis=4, concat_axis...]
    dot_general x32 -> x0, matrix products: 42.3 us -> none  [the longest x8 19.7 us: spectra_of(): jnp.einsum('cft,stkx->scfkx', time_basis, segment, preferred_element_type...]
    another operation x1 -> x0, loops' own time: 15.6 us -> none  [local(): spectra = lax.map(spectra_of, own_starts)]
    reduce_sum x65 -> x0, other arithmetic: 15 us -> none  [the longest x32 9.13 us: subspace(): proj_re = jnp.sum(old_re * vec_re + old_im * vec_im, -1, keepdims=True)]
    all_to_all x2 -> x0, starting transfers between devices: 13.8 us -> none  [the longest x1 9.61 us: local(): lax.all_to_all(spectra[None], ('sector', 'tm'), split_axis=4, concat_axis...]
    while x1 -> x0, local copies, waits for them, and re-layouts: 8.89 us -> none  [local(): spectra = lax.map(spectra_of, own_starts)]
    dynamic_slice x9 -> x0, local copies, waits for them, and re-layouts: 5.39 us -> none  [the longest x8 4.66 us: local(): spectra = lax.map(spectra_of, own_starts)]
  transfers between devices with their start and end apart: 2 -> 0, of which waited for: 2 -> 0; matrix products, arithmetic and copies ran while one was open for 0% -> 0% of each run, Pallas kernels for 0% -> 0%
where the time goes in v1:
time: 100 us; the launch traced here: 99.8 us
  Pallas kernels  95.2 us (95%)
  local copies, waits for them, and re-layouts  3.99 us (4%)
    pallas_call x1, Pallas kernels, local(): pl.pallas_call(gather_kernel, name='gather', out_shape=(jax.ShapeDtypeStr...  86.3 us
    pallas_call x1, Pallas kernels, local(): pl.pallas_call(modes_kernel, name='modes', out_shape=(jax.ShapeDtypeStruc...  8.9 us
    unnamed x10, local copies, waits for them, and re-layouts  3.99 us

profile of v1, /device:TPU:1, one launch (start us, length us, event | category | flops | bytes accessed | tf_op | source)
XLA Modules:
  0.0 99.8 jit_solution(9439503592778439396)
XLA Ops:
  0.6 0.0 copy-start
  0.6 1.0 %copy-done = bf16[512,512]{1,0:T(8,128)(2,1)S(1)} copy-done((bf16[512,512]{1,0:T(8,128)(2,1)S(1)}, bf16[512,512]{1,0:T(8,128)(2,1)}, u32[]{:S(2)}) %copy-start) | copy-done | bytes 524312
  1.7 0.0 copy-start.1
  1.7 0.9 copy-done.1
  2.6 0.0 copy-start.2
  2.6 0.7 copy-done.2
  3.3 0.0 copy-start.3
  3.3 0.7 copy-done.3
  4.0 0.0 copy-start.4
  4.0 0.7 copy-done.4
  4.6 86.3 %gather.1 = (bf16[3,256,2048]{2,1,0:T(8,128)(2,1)S(1)}, f32[2,16,128]{2,1,0:T(8,128)S(1)}) custom-call(bf16[3,296,2048]{2,1,0:T(8,128)(2,1)} %bitcast.11, s32[16]{0:T(128)S(1)} %copy-done.4, f32[16]{0:T(128)S(1)} %copy-done.3, s32[1,2048]{1,0:T(1,128)S(1)} %bitcast.9, bf16[512,512]{1,0:T(8,128)(2,1)S(1)} %copy-done, bf16[256,512]{1,0:T(8,128)(2,1)S(1)} %copy-done.1), custom_call_target="tpu_custom_call" | custom-call | tf_op jit(solution)/shard_map/gather/pallas_call | solution.py:346
  90.9 8.9 %modes.1 = (bf16[16,3,8,2048]{3,2,1,0:T(8,128)(2,1)}, f32[8,1,8]{2,1,0:T(1,128)}) custom-call(bf16[3,256,2048]{2,1,0:T(8,128)(2,1)S(1)} %get-tuple-element.6.coef_hbm, f32[2,16,128]{2,1,0:T(8,128)S(1)} %get-tuple-element.7.gram_ref, f32[16]{0:T(128)S(1)} %copy-done.3, s32[1,2048]{1,0:T(1,128)S(1)} %bitcast.10), custom_call_target="tpu_custom_call" | custom-call | tf_op jit(solution)/shard_map/modes/pallas_call | solution.py:377
Async XLA Ops:
  0.6 1.0 %copy-start = (bf16[512,512]{1,0:T(8,128)(2,1)S(1)}, bf16[512,512]{1,0:T(8,128)(2,1)}, u32[]{:S(2)}) copy-start(bf16[512,512]{1,0:T(8,128)(2,1)} %constant.4.clone.basis_ref) | copy-start | bytes 1572868
  1.7 0.9 copy-start.1
  2.6 0.7 copy-start.2
  3.3 0.7 copy-start.3
  4.0 0.7 copy-start.4

commit v2 on v1

--- a/solution.py
+++ b/solution.py
@@ -32,6 +32,8 @@
 ROWS = 2 * BLK
 LANES = 128
 TILE = 512
+WIDE = 1024
+CHUNKS = ((0, 0, 512), (0, 512, 1536), (1, 0, 2048), (2, 0, 1536), (2, 1536, 512))
 
 
 def time_table():
@@ -105,9 +107,9 @@
 
 
 def gather_kernel(
-    rec_hbm, start_ref, table_ref, slab_ref, basis_ref, order_ref, coef_hbm, gram_ref,
-    rec, send, recv, coef, band, shift, weight, acc, slots,
-    rec_sem, own_sem, send_sem, recv_sem, coef_sem, gsend_sem, grecv_sem,
+    rec_hbm, start_hbm, table_hbm, slab_hbm, basis_hbm, order_hbm, coef, gram_ref, weight,
+    rec, send, recv, start, table, slab, basis, mixer, band, shift, acc, slots,
+    in_sem, rec_sem, own_sem, send_sem, recv_sem, gsend_sem, grecv_sem,
 ):
     x, y, z, core = place()
     tm = x // 2
@@ -124,42 +126,53 @@
         pl.semaphore_signal(
             barrier, inc=1, device_id=device_at(x, (y + d) % SPACE, z, core), device_id_type=MESH
         )
+    pairs = (
+        (start_hbm, start), (basis_hbm, basis), (slab_hbm, slab), (table_hbm, table),
+        (order_hbm, mixer),
+    )
+    smalls = [
+        pltpu.make_async_copy(src, dst, in_sem.at[n]) for n, (src, dst) in enumerate(pairs)
+    ]
     loads = [
-        pltpu.make_async_copy(rec_hbm.at[k], rec.at[k], rec_sem.at[k]) for k in range(FIELDS)
+        pltpu.make_async_copy(
+            rec_hbm.at[k, :, pl.ds(first, size)], rec.at[k, :, pl.ds(first, size)], rec_sem.at[n]
+        )
+        for n, (k, first, size) in enumerate(CHUNKS)
     ]
-    for load in loads:
+    for load in (smalls[0], smalls[1], loads[0], *loads[1:], *smalls[2:]):
         load.start()
-
-    weight[...] = weight_row(slab_ref, table_ref)
+    smalls[0].wait()
     step = lax.broadcasted_iota(jnp.int32, (NFFT, TREC), 1) - lax.broadcasted_iota(
         jnp.int32, (NFFT, TREC), 0
     )
     for b in range(BLK):
         shift[b * NFFT : (b + 1) * NFFT, :] = jnp.where(
-            step == start_ref[tm * BLK + b], 1.0, 0.0
+            step == start[tm * BLK + b], 1.0, 0.0
         ).astype(BF)
-    band[...] = jnp.dot(basis_ref[...], shift[...], preferred_element_type=F32).astype(BF)
+    smalls[1].wait()
+    band[...] = jnp.dot(basis[...], shift[...], preferred_element_type=F32).astype(BF)
 
     copies, owns = [], []
-    for k in range(FIELDS):
-        loads[k].wait()
-
-        @pl.loop(0, CELLS // TILE)
+    for n, (k, first, size) in enumerate(CHUNKS):
+        loads[n].wait()
+
+        @pl.loop(0, size // TILE)
         def _(t):
-            cols = pl.ds(pl.multiple_of(t * TILE, TILE), TILE)
+            cols = pl.ds(pl.multiple_of(first + t * TILE, TILE), TILE)
             out = jnp.dot(band[...], rec[k, :, cols], preferred_element_type=F32)
             send[k, :, :, cols] = out.astype(BF).reshape(NFREQ, ROWS, TILE)
 
-        if k == 0:
+        if n == 0:
             pl.semaphore_wait(barrier, len(ORDER) + SPACE - 1)
+        span = pl.ds(first, size)
         for i, offset in enumerate(ORDER):
             px, py, pz, pc = peer(offset)
             sector, ptm, _ = device_at(px, py, pz, pc)
             copy = pltpu.make_async_remote_copy(
-                src_ref=send.at[k, sector * TMS + ptm],
-                dst_ref=recv.at[k, own],
-                send_sem=send_sem.at[k, i],
-                recv_sem=recv_sem.at[k, i],
+                src_ref=send.at[k, sector * TMS + ptm, :, span],
+                dst_ref=recv.at[k, own, :, span],
+                send_sem=send_sem.at[n, i],
+                recv_sem=recv_sem.at[n, i],
                 device_id=device_at(px, py, pz, pc),
                 device_id_type=MESH,
             )
@@ -167,32 +180,30 @@
             copies.append(copy)
         sector, ptm, _ = device_at(x, y, z, core)
         mine = pltpu.make_async_copy(
-            send.at[k, sector * TMS + ptm], recv.at[k, own], own_sem.at[k]
+            send.at[k, sector * TMS + ptm, :, span], recv.at[k, own, :, span], own_sem.at[n]
         )
         mine.start()
         owns.append(mine)
 
+    for small in smalls[2:]:
+        small.wait()
+    weight[...] = weight_row(slab, table)
     acc[...] = jnp.zeros_like(acc)
-    stores = []
-    for k in range(FIELDS):
-        for copy in copies[k * len(ORDER) : (k + 1) * len(ORDER)]:
+    for n, (k, first, size) in enumerate(CHUNKS):
+        for copy in copies[n * len(ORDER) : (n + 1) * len(ORDER)]:
             copy.wait_recv()
-        owns[k].wait()
-
-        @pl.loop(0, CELLS // TILE)
+        owns[n].wait()
+
+        @pl.loop(0, size // TILE)
         def _(t):
-            cols = pl.ds(pl.multiple_of(t * TILE, TILE), TILE)
+            cols = pl.ds(pl.multiple_of(first + t * TILE, TILE), TILE)
             arrived = recv[k, :, :, cols].reshape(SLOTS * ROWS, TILE)
-            c = jnp.dot(order_ref[...], arrived, preferred_element_type=F32).astype(BF)
+            c = jnp.dot(mixer[...], arrived, preferred_element_type=F32).astype(BF)
             coef[k, :, cols] = c
             weighted = (c.astype(F32) * weight[:, cols]).astype(BF)
             acc[...] += lax.dot_general(
                 weighted, c, (((1,), (1,)), ((), ())), preferred_element_type=F32
             )
-
-        store = pltpu.make_async_copy(coef.at[k], coef_hbm.at[k], coef_sem.at[k])
-        store.start()
-        stores.append(store)
 
     half = ORDERS * BLOCKS
     full_re = acc[:half, :half] + acc[half:, half:]
@@ -225,8 +236,6 @@
         swap.wait_send()
     for copy in copies:
         copy.wait_send()
-    for store in stores:
-        store.wait()
 
 
 def take(array, index):
@@ -234,15 +243,9 @@
 
 
 def modes_kernel(
-    coef_hbm, gram_ref, table_ref, slab_ref, out_hbm, energy_ref,
-    coef, out, mix, scale, root, coef_sem, out_sem,
+    coef, gram_ref, weight, out_hbm, energy_ref, out, mix, scale, root, out_sem,
 ):
-    loads = [
-        pltpu.make_async_copy(coef_hbm.at[k], coef.at[k], coef_sem.at[k]) for k in range(FIELDS)
-    ]
-    for load in loads:
-        load.start()
-    root[...] = jnp.sqrt(weight_row(slab_ref, table_ref))
+    root[...] = jnp.sqrt(weight[...])
 
     shape = (BLOCKS, LANES)
     lane = lax.broadcasted_iota(jnp.int32, shape, 1)
@@ -277,10 +280,10 @@
         for i in range(MODES):
             index = order + i * ORDERS
             v_re, v_im = take(re, index), take(im, index)
-            size = total(v_re * v_re + v_im * v_im) + EPSILON
-            q_re = total(v_re * re + v_im * im) / size
-            q_im = total(v_re * im - v_im * re) / size
-            norm = lax.rsqrt(size)
+            norm = lax.rsqrt(total(v_re * v_re + v_im * v_im) + EPSILON)
+            inverse = norm * norm
+            q_re = total(v_re * re + v_im * im) * inverse
+            q_im = total(v_re * im - v_im * re) * inverse
             later, here = column > i, column == i
             re, im = (
                 jnp.where(
@@ -312,19 +315,18 @@
         block = jnp.where(diagonal, jnp.concatenate([part] * ORDERS, 0), 0.0)
         mix[:, c * LANES : (c + 1) * LANES] = block.T.astype(BF)
     factor = jnp.broadcast_to(lax.rsqrt(take(energy, target))[:1], (LANES, LANES)).T
-    for n in range(TILE // LANES):
+    for n in range(WIDE // LANES):
         scale[:, n * LANES : (n + 1) * LANES] = factor
 
     stores = []
     for k in range(FIELDS):
-        loads[k].wait()
-
-        @pl.loop(0, CELLS // TILE)
+
+        @pl.loop(0, CELLS // WIDE)
         def _(t):
-            cols = pl.ds(pl.multiple_of(t * TILE, TILE), TILE)
+            cols = pl.ds(pl.multiple_of(t * WIDE, WIDE), WIDE)
             fields = jnp.dot(mix[...], coef[k, :, cols], preferred_element_type=F32)
             fields = fields * (scale[...] * root[:, cols])
-            out[:, k, :, cols] = fields.astype(BF).reshape(2 * ORDERS, MODES, TILE)
+            out[:, k, :, cols] = fields.astype(BF).reshape(2 * ORDERS, MODES, WIDE)
 
         store = pltpu.make_async_copy(out.at[:, k], out_hbm.at[:, k], out_sem.at[k])
         store.start()
@@ -337,43 +339,50 @@
     assert records.shape == (1, TREC, FIELDS, CELLS)
     rec = jnp.transpose(records[0], (1, 0, 2))
     slab = slab_index.reshape(1, CELLS)
-    any_spec = pl.BlockSpec(memory_space=pl.ANY)
-    smem = pl.BlockSpec(memory_space=pltpu.SMEM)
+    hbm = pl.BlockSpec(memory_space=pltpu.HBM)
     vmem = pl.BlockSpec(memory_space=pltpu.VMEM)
     dma = pltpu.SemaphoreType.DMA
     width = 2 * ORDERS * BLOCKS
-    count = len(ORDER)
-    coef, gram = pl.pallas_call(
+    count, chunks = len(ORDER), len(CHUNKS)
+    basis, mixer = spread_time_table(), spread_order_table()
+    coef, gram, weight = pl.pallas_call(
         gather_kernel,
         name="gather",
         out_shape=(
             jax.ShapeDtypeStruct((FIELDS, width, CELLS), BF),
             jax.ShapeDtypeStruct((2, BLOCKS, LANES), F32),
+            jax.ShapeDtypeStruct((1, CELLS), F32),
         ),
-        in_specs=[any_spec, smem, smem, vmem, vmem, vmem],
-        out_specs=(any_spec, vmem),
+        in_specs=[hbm] * 6,
+        out_specs=(vmem, vmem, vmem),
         scratch_shapes=[
             pltpu.VMEM((FIELDS, TREC, CELLS), BF),
             pltpu.VMEM((FIELDS, NFREQ, ROWS, CELLS), BF),
             pltpu.VMEM((FIELDS, SLOTS, ROWS, CELLS), BF),
-            pltpu.VMEM((FIELDS, width, CELLS), BF),
+            pltpu.SMEM((BLOCKS,), jnp.int32),
+            pltpu.SMEM((NSLAB,), F32),
+            pltpu.VMEM((1, CELLS), jnp.int32),
+            pltpu.VMEM(basis.shape, BF),
+            pltpu.VMEM(mixer.shape, BF),
             pltpu.VMEM((NFREQ * ROWS, TREC), BF),
             pltpu.VMEM((BLK * NFFT, TREC), BF),
-            pltpu.VMEM((1, CELLS), F32),
             pltpu.VMEM((width, width), F32),
             pltpu.VMEM((SPACE, 2, BLOCKS, LANES), F32),
-            dma((FIELDS,)),
-            dma((FIELDS,)),
-            dma((FIELDS, count)),
-            dma((FIELDS, count)),
-            dma((FIELDS,)),
+            dma((5,)),
+            dma((chunks,)),
+            dma((chunks,)),
+            dma((chunks, count)),
+            dma((chunks, count)),
             dma((SPACE - 1,)),
             dma((SPACE - 1,)),
         ],
         compiler_params=pltpu.CompilerParams(
-            collective_id=0, has_side_effects=True, vmem_limit_bytes=48 << 20
+            collective_id=0, has_side_effects=True, vmem_limit_bytes=40 << 20
         ),
-    )(rec, block_start, weight_table, slab, jnp.asarray(spread_time_table()), jnp.asarray(spread_order_table()))
+    )(*(
+        pltpu.with_memory_space_constraint(a, pltpu.HBM)
+        for a in (rec, block_start, weight_table, slab, jnp.asarray(basis), jnp.asarray(mixer))
+    ))
     out, energy = pl.pallas_call(
         modes_kernel,
         name="modes",
@@ -381,19 +390,17 @@
             jax.ShapeDtypeStruct((2 * ORDERS, FIELDS, MODES, CELLS), BF),
             jax.ShapeDtypeStruct((ORDERS, 1, MODES), F32),
         ),
-        in_specs=[any_spec, vmem, smem, vmem],
-        out_specs=(any_spec, vmem),
+        in_specs=[vmem, vmem, vmem],
+        out_specs=(hbm, vmem),
         scratch_shapes=[
-            pltpu.VMEM((FIELDS, width, CELLS), BF),
             pltpu.VMEM((2 * ORDERS, FIELDS, MODES, CELLS), BF),
             pltpu.VMEM((LANES, width), BF),
-            pltpu.VMEM((LANES, TILE), F32),
+            pltpu.VMEM((LANES, WIDE), F32),
             pltpu.VMEM((1, CELLS), F32),
             dma((FIELDS,)),
-            dma((FIELDS,)),
         ],
-        compiler_params=pltpu.CompilerParams(vmem_limit_bytes=32 << 20),
-    )(coef, gram, weight_table, slab)
+        compiler_params=pltpu.CompilerParams(vmem_limit_bytes=24 << 20),
+    )(coef, gram, weight)
     out = out.reshape(ORDERS, 1, 2, FIELDS, MODES, CELLS)
     return jnp.transpose(out, (0, 1, 2, 4, 3, 5)), energy
 

time: 100 us -> 93.5 us (0.935)
  local copies, waits for them, and re-layouts: 3.99 us -> 0 us
  Pallas kernels: 95.2 us -> 92.8 us
    unnamed x10 -> x0, local copies, waits for them, and re-layouts: 3.99 us -> none
    pallas_call x1, Pallas kernels: 8.9 us -> 7.25 us  [local(): pl.pallas_call(modes_kernel, name='modes', out_shape=(jax.ShapeDtypeStruc...]
where the time goes in v2:
time: 93.5 us; the launch traced here: 93.4 us
  Pallas kernels  92.8 us (99%)
    pallas_call x1, Pallas kernels, local(): pl.pallas_call(gather_kernel, name='gather', out_shape=(jax.ShapeDtypeStr...  85.5 us
    pallas_call x1, Pallas kernels, local(): pl.pallas_call(modes_kernel, name='modes', out_shape=(jax.ShapeDtypeStruc...  7.25 us

profile of v2, /device:TPU:1, one launch (start us, length us, event | category | flops | bytes accessed | tf_op | source)
XLA Modules:
  0.0 93.4 jit_solution(14610340173824963666)
XLA Ops:
  0.6 85.5 %gather.1 = (bf16[3,256,2048]{2,1,0:T(8,128)(2,1)S(1)}, f32[2,16,128]{2,1,0:T(8,128)S(1)}, f32[1,2048]{1,0:T(1,128)S(1)}) custom-call(bf16[3,296,2048]{2,1,0:T(8,128)(2,1)} %bitcast.9, s32[16]{0:T(128)} %start_hbm.1, f32[16]{0:T(128)} %table_hbm.1, s32[1,2048]{1,0:T(1,128)} %bitcast.10, bf16[512,512]{1,0:T(8,128)(2,1)} %constant.4.clone.basis_hbm, ...), custom_call_target="tpu_custom_call" | custom-call | tf_op jit(solution)/shard_map/gather/pallas_call | solution.py:348
  86.2 7.3 %modes.1 = (bf16[16,3,8,2048]{3,2,1,0:T(8,128)(2,1)}, f32[8,1,8]{2,1,0:T(1,128)}) custom-call(bf16[3,256,2048]{2,1,0:T(8,128)(2,1)S(1)} %get-tuple-element.7.coef, f32[2,16,128]{2,1,0:T(8,128)S(1)} %get-tuple-element.8.gram_ref, f32[1,2048]{1,0:T(1,128)S(1)} %get-tuple-element.9.weight), custom_call_target="tpu_custom_call" | custom-call | tf_op jit(solution)/shard_map/modes/pallas_call | solution.py:386

commit v3 on v2

--- a/solution.py
+++ b/solution.py
@@ -32,7 +32,7 @@
 ROWS = 2 * BLK
 LANES = 128
 TILE = 512
-WIDE = 1024
+WIDE = 2048
 CHUNKS = ((0, 0, 512), (0, 512, 1536), (1, 0, 2048), (2, 0, 1536), (2, 1536, 512))
 
 
@@ -249,25 +249,28 @@
 
     shape = (BLOCKS, LANES)
     lane = lax.broadcasted_iota(jnp.int32, shape, 1)
-    low = lane < LANES // 2
     column = (lane // ORDERS) % MODES
     order = lane % ORDERS
     gram_re, gram_im = gram_ref[0], gram_ref[1]
-    both = jnp.concatenate([gram_re, gram_im], 0)
     wide = (BLOCKS * ORDERS, LANES)
-    same = (
-        lax.broadcasted_iota(jnp.int32, wide, 0) // BLOCKS
-        == lax.broadcasted_iota(jnp.int32, wide, 1) % ORDERS
-    )
+    grid = [
+        (take(gram_re, order * BLOCKS + e), take(gram_im, order * BLOCKS + e))
+        for e in range(BLOCKS)
+    ]
+
+    def added(terms):
+        while len(terms) > 1:
+            terms = [sum(terms[n : n + 2]) for n in range(0, len(terms), 2)]
+        return terms[0]
 
     def apply(re, im):
-        right = jnp.where(same, jnp.concatenate([jnp.where(low, re, im)] * ORDERS, 0), 0.0)
-        image = jnp.dot(
-            both, right, preferred_element_type=F32, precision=lax.Precision.HIGHEST
+        parts = [
+            (g_re, g_im, re[e : e + 1], im[e : e + 1]) for e, (g_re, g_im) in enumerate(grid)
+        ]
+        return (
+            added([g_re * v_re - g_im * v_im for g_re, g_im, v_re, v_im in parts]),
+            added([g_re * v_im + g_im * v_re for g_re, g_im, v_re, v_im in parts]),
         )
-        turned = pltpu.roll(image, LANES // 2, 1)
-        p0, p1, t0, t1 = image[:BLOCKS], image[BLOCKS:], turned[:BLOCKS], turned[BLOCKS:]
-        return jnp.where(low, p0 - t1, t0 - p1), jnp.where(low, t0 + p1, p0 + t1)
 
     def total(a):
         return jnp.sum(a, axis=0, keepdims=True)
@@ -277,21 +280,25 @@
     for sweep in range(SUBIT):
         if sweep:
             re, im = apply(re, im)
+        columns = [
+            (take(re, order + i * ORDERS), take(im, order + i * ORDERS)) for i in range(MODES)
+        ]
         for i in range(MODES):
-            index = order + i * ORDERS
-            v_re, v_im = take(re, index), take(im, index)
+            v_re, v_im = columns[i]
             norm = lax.rsqrt(total(v_re * v_re + v_im * v_im) + EPSILON)
             inverse = norm * norm
-            q_re = total(v_re * re + v_im * im) * inverse
-            q_im = total(v_re * im - v_im * re) * inverse
-            later, here = column > i, column == i
+            for j in range(i + 1, MODES):
+                u_re, u_im = columns[j]
+                q_re = total(v_re * u_re + v_im * u_im) * inverse
+                q_im = total(v_re * u_im - v_im * u_re) * inverse
+                columns[j] = (
+                    u_re - (q_re * v_re - q_im * v_im), u_im - (q_re * v_im + q_im * v_re)
+                )
+            columns[i] = v_re * norm, v_im * norm
+        re, im = columns[0]
+        for i in range(1, MODES):
             re, im = (
-                jnp.where(
-                    later, re - (q_re * v_re - q_im * v_im), jnp.where(here, v_re * norm, re)
-                ),
-                jnp.where(
-                    later, im - (q_re * v_im + q_im * v_re), jnp.where(here, v_im * norm, im)
-                ),
+                jnp.where(column == i, columns[i][0], re), jnp.where(column == i, columns[i][1], im)
             )
     image_re, image_im = apply(re, im)
     energy = total(re * image_re + im * image_im) * (1.0 / (FIELDS * CELLS * SPACE))

time: 93.5 us -> 90 us (0.963)
  Pallas kernels: 92.8 us -> 89.2 us
    pallas_call x1, Pallas kernels: 7.25 us -> 3.67 us  [local(): pl.pallas_call(modes_kernel, name='modes', out_shape=(jax.ShapeDtypeStruc...]
where the time goes in v3:
time: 90 us; the launch traced here: 89.8 us
  Pallas kernels  89.2 us (99%)
    pallas_call x1, Pallas kernels, local(): pl.pallas_call(gather_kernel, name='gather', out_shape=(jax.ShapeDtypeStr...  85.5 us
    pallas_call x1, Pallas kernels, local(): pl.pallas_call(modes_kernel, name='modes', out_shape=(jax.ShapeDtypeStruc...  3.67 us

profile of v3, /device:TPU:1, one launch (start us, length us, event | category | flops | bytes accessed | tf_op | source)
XLA Modules:
  0.0 89.8 jit_solution(3515711845257641387)
XLA Ops:
  0.6 85.5 %gather.1 = (bf16[3,256,2048]{2,1,0:T(8,128)(2,1)S(1)}, f32[2,16,128]{2,1,0:T(8,128)S(1)}, f32[1,2048]{1,0:T(1,128)S(1)}) custom-call(bf16[3,296,2048]{2,1,0:T(8,128)(2,1)} %bitcast.9, s32[16]{0:T(128)} %start_hbm.1, f32[16]{0:T(128)} %table_hbm.1, s32[1,2048]{1,0:T(1,128)} %bitcast.10, bf16[512,512]{1,0:T(8,128)(2,1)} %constant.4.clone.basis_hbm, ...), custom_call_target="tpu_custom_call" | custom-call | tf_op jit(solution)/shard_map/gather/pallas_call | solution.py:355
  86.2 3.7 %modes.1 = (bf16[16,3,8,2048]{3,2,1,0:T(8,128)(2,1)}, f32[8,1,8]{2,1,0:T(1,128)}) custom-call(bf16[3,256,2048]{2,1,0:T(8,128)(2,1)S(1)} %get-tuple-element.7.coef, f32[2,16,128]{2,1,0:T(8,128)S(1)} %get-tuple-element.8.gram_ref, f32[1,2048]{1,0:T(1,128)S(1)} %get-tuple-element.9.weight), custom_call_target="tpu_custom_call" | custom-call | tf_op jit(solution)/shard_map/modes/pallas_call | solution.py:393

commit v4 on v3

--- a/solution.py
+++ b/solution.py
@@ -31,9 +31,8 @@
 SLOTS = TMS * SECTORS
 ROWS = 2 * BLK
 LANES = 128
-TILE = 512
 WIDE = 2048
-CHUNKS = ((0, 0, 512), (0, 512, 1536), (1, 0, 2048), (2, 0, 1536), (2, 1536, 512))
+CHUNKS = ((0, 0, 2048), (1, 0, 2048), (2, 0, 2048))
 
 
 def time_table():
@@ -155,16 +154,12 @@
     copies, owns = [], []
     for n, (k, first, size) in enumerate(CHUNKS):
         loads[n].wait()
-
-        @pl.loop(0, size // TILE)
-        def _(t):
-            cols = pl.ds(pl.multiple_of(first + t * TILE, TILE), TILE)
-            out = jnp.dot(band[...], rec[k, :, cols], preferred_element_type=F32)
-            send[k, :, :, cols] = out.astype(BF).reshape(NFREQ, ROWS, TILE)
+        span = pl.ds(first, size)
+        out = jnp.dot(band[...], rec[k, :, span], preferred_element_type=F32)
+        send[k, :, :, span] = out.astype(BF).reshape(NFREQ, ROWS, size)
 
         if n == 0:
             pl.semaphore_wait(barrier, len(ORDER) + SPACE - 1)
-        span = pl.ds(first, size)
         for i, offset in enumerate(ORDER):
             px, py, pz, pc = peer(offset)
             sector, ptm, _ = device_at(px, py, pz, pc)
@@ -193,17 +188,14 @@
         for copy in copies[n * len(ORDER) : (n + 1) * len(ORDER)]:
             copy.wait_recv()
         owns[n].wait()
-
-        @pl.loop(0, size // TILE)
-        def _(t):
-            cols = pl.ds(pl.multiple_of(first + t * TILE, TILE), TILE)
-            arrived = recv[k, :, :, cols].reshape(SLOTS * ROWS, TILE)
-            c = jnp.dot(mixer[...], arrived, preferred_element_type=F32).astype(BF)
-            coef[k, :, cols] = c
-            weighted = (c.astype(F32) * weight[:, cols]).astype(BF)
-            acc[...] += lax.dot_general(
-                weighted, c, (((1,), (1,)), ((), ())), preferred_element_type=F32
-            )
+        span = pl.ds(first, size)
+        arrived = recv[k, :, :, span].reshape(SLOTS * ROWS, size)
+        c = jnp.dot(mixer[...], arrived, preferred_element_type=F32).astype(BF)
+        coef[k, :, span] = c
+        weighted = (c.astype(F32) * weight[:, span]).astype(BF)
+        acc[...] += lax.dot_general(
+            weighted, c, (((1,), (1,)), ((), ())), preferred_element_type=F32
+        )
 
     half = ORDERS * BLOCKS
     full_re = acc[:half, :half] + acc[half:, half:]
@@ -229,13 +221,13 @@
         )
         swap.start()
         swaps.append(swap)
+    for copy in copies:
+        copy.wait_send()
     for swap in swaps:
         swap.wait_recv()
     gram_ref[...] = (slots[0] + slots[1]) + (slots[2] + slots[3])
     for swap in swaps:
         swap.wait_send()
-    for copy in copies:
-        copy.wait_send()
 
 
 def take(array, index):
@@ -277,9 +269,7 @@
 
     first = order * BLOCKS + column
     re, im = take(gram_re, first), take(gram_im, first)
-    for sweep in range(SUBIT):
-        if sweep:
-            re, im = apply(re, im)
+    def sweep(re, im):
         columns = [
             (take(re, order + i * ORDERS), take(im, order + i * ORDERS)) for i in range(MODES)
         ]
@@ -300,6 +290,10 @@
             re, im = (
                 jnp.where(column == i, columns[i][0], re), jnp.where(column == i, columns[i][1], im)
             )
+        return re, im
+
+    re, im = sweep(re, im)
+    re, im = lax.fori_loop(1, SUBIT, lambda _, basis: sweep(*apply(*basis)), (re, im))
     image_re, image_im = apply(re, im)
     energy = total(re * image_re + im * image_im) * (1.0 / (FIELDS * CELLS * SPACE))
     energy = jnp.broadcast_to(energy, shape)

time: 90 us -> 89.1 us (0.990)
  Pallas kernels: 89.2 us -> 88.3 us
where the time goes in v4:
time: 89.1 us; the launch traced here: 89 us
  Pallas kernels  88.3 us (99%)
    pallas_call x1, Pallas kernels, local(): pl.pallas_call(gather_kernel, name='gather', out_shape=(jax.ShapeDtypeStr...  84.7 us
    pallas_call x1, Pallas kernels, local(): pl.pallas_call(modes_kernel, name='modes', out_shape=(jax.ShapeDtypeStruc...  3.69 us

profile of v4, /device:TPU:1, one launch (start us, length us, event | category | flops | bytes accessed | tf_op | source)
XLA Modules:
  0.0 89.0 jit_solution(7293914610595929404)
XLA Ops:
  0.6 84.7 %gather.1 = (bf16[3,256,2048]{2,1,0:T(8,128)(2,1)S(1)}, f32[2,16,128]{2,1,0:T(8,128)S(1)}, f32[1,2048]{1,0:T(1,128)S(1)}) custom-call(bf16[3,296,2048]{2,1,0:T(8,128)(2,1)} %bitcast.9, s32[16]{0:T(128)} %start_hbm.1, f32[16]{0:T(128)} %table_hbm.1, s32[1,2048]{1,0:T(1,128)} %bitcast.10, bf16[512,512]{1,0:T(8,128)(2,1)} %constant.4.clone.basis_hbm, ...), custom_call_target="tpu_custom_call" | custom-call | tf_op jit(solution)/shard_map/gather/pallas_call | solution.py:349
  85.3 3.7 %modes.1 = (bf16[16,3,8,2048]{3,2,1,0:T(8,128)(2,1)}, f32[8,1,8]{2,1,0:T(1,128)}) custom-call(bf16[3,256,2048]{2,1,0:T(8,128)(2,1)S(1)} %get-tuple-element.7.coef, f32[2,16,128]{2,1,0:T(8,128)S(1)} %get-tuple-element.8.gram_ref, f32[1,2048]{1,0:T(1,128)S(1)} %get-tuple-element.9.weight), custom_call_target="tpu_custom_call" | custom-call | tf_op jit(solution)/shard_map/modes/pallas_call | solution.py:387

commit v5 on v4

--- a/solution.py
+++ b/solution.py
@@ -81,17 +81,17 @@
 
 
 def send_order():
-    dist = (0, 1, 2, 1)
-    offsets = [
-        (a, b, c) for a in range(4) for b in range(4) for c in range(2) if (a, b, c) != (0, 0, 0)
+    far_z, far_x = ((1, 2), (3, 2)), ((2, 1), (2, 3))
+    only_x, only_z = ((2, 0),), ((0, 2),)
+    common = (
+        (1, 1), (3, 3), (1, 3), (3, 1), (2, 2), (1, 0), (3, 0), (0, 1), (0, 3),
+    )
+    zero = (*far_z, *only_x, *far_x, *only_z, *common)
+    one = (*far_x, *only_z, *far_z, *only_x, *common)
+    steps = [
+        ((*o, c), (*p, 1 - c)) for c in range(2) for o, p in zip(zero, one, strict=True)
     ]
-    offsets.sort(key=lambda o: -(dist[o[0]] + dist[o[1]]))
-    order = []
-    for a, b, c in offsets:
-        for o in ((a, b, c), (-a % 4, -b % 4, c), (b, a, c), (-b % 4, -a % 4, c)):
-            if o not in order:
-                order.append(o)
-    return order
+    return [*steps, ((0, 0, 1), (0, 0, 1))]
 
 
 ORDER = send_order()
@@ -114,9 +114,16 @@
     tm = x // 2
     own = tm * SECTORS + z * 4 + (x % 2) * 2 + core
 
-    def peer(offset):
-        a, b, c = offset
-        return (x + a + core * (b - a)) % 4, y, (z + b + core * (a - b)) % 4, (core + c) % 2
+    def own_offset(step):
+        return tuple(p + core * (q - p) for p, q in zip(*step))
+
+    def peer(step):
+        a, b, c = own_offset(step)
+        return (x + a) % 4, y, (z + b) % 4, (core + c) % 2
+
+    def slot_of(step):
+        a, b, c = own_offset(step)
+        return a * 8 + b * 2 + c
 
     barrier = pltpu.get_barrier_semaphore()
     for offset in ORDER:
@@ -160,14 +167,14 @@
 
         if n == 0:
             pl.semaphore_wait(barrier, len(ORDER) + SPACE - 1)
-        for i, offset in enumerate(ORDER):
+        for offset in ORDER:
             px, py, pz, pc = peer(offset)
             sector, ptm, _ = device_at(px, py, pz, pc)
             copy = pltpu.make_async_remote_copy(
                 src_ref=send.at[k, sector * TMS + ptm, :, span],
                 dst_ref=recv.at[k, own, :, span],
-                send_sem=send_sem.at[n, i],
-                recv_sem=recv_sem.at[n, i],
+                send_sem=send_sem.at[n, slot_of(offset)],
+                recv_sem=recv_sem.at[n, slot_of(offset)],
                 device_id=device_at(px, py, pz, pc),
                 device_id_type=MESH,
             )
@@ -344,7 +351,7 @@
     vmem = pl.BlockSpec(memory_space=pltpu.VMEM)
     dma = pltpu.SemaphoreType.DMA
     width = 2 * ORDERS * BLOCKS
-    count, chunks = len(ORDER), len(CHUNKS)
+    chunks = len(CHUNKS)
     basis, mixer = spread_time_table(), spread_order_table()
     coef, gram, weight = pl.pallas_call(
         gather_kernel,
@@ -372,8 +379,8 @@
             dma((5,)),
             dma((chunks,)),
             dma((chunks,)),
-            dma((chunks, count)),
-            dma((chunks, count)),
+            dma((chunks, SLOTS)),
+            dma((chunks, SLOTS)),
             dma((SPACE - 1,)),
             dma((SPACE - 1,)),
         ],

time: 89.1 us -> 90 us (1.010)
  Pallas kernels: 88.3 us -> 89.2 us
where the time goes in v5:
time: 90 us; the launch traced here: 89.9 us
  Pallas kernels  89.2 us (99%)
    pallas_call x1, Pallas kernels, local(): pl.pallas_call(gather_kernel, name='gather', out_shape=(jax.ShapeDtypeStr...  85.5 us
    pallas_call x1, Pallas kernels, local(): pl.pallas_call(modes_kernel, name='modes', out_shape=(jax.ShapeDtypeStruc...  3.69 us

profile of v5, /device:TPU:1, one launch (start us, length us, event | category | flops | bytes accessed | tf_op | source)
XLA Modules:
  0.0 89.9 jit_solution(14864980022119279288)
XLA Ops:
  0.6 85.5 %gather.1 = (bf16[3,256,2048]{2,1,0:T(8,128)(2,1)S(1)}, f32[2,16,128]{2,1,0:T(8,128)S(1)}, f32[1,2048]{1,0:T(1,128)S(1)}) custom-call(bf16[3,296,2048]{2,1,0:T(8,128)(2,1)} %bitcast.9, s32[16]{0:T(128)} %start_hbm.1, f32[16]{0:T(128)} %table_hbm.1, s32[1,2048]{1,0:T(1,128)} %bitcast.10, bf16[512,512]{1,0:T(8,128)(2,1)} %constant.4.clone.basis_hbm, ...), custom_call_target="tpu_custom_call" | custom-call | tf_op jit(solution)/shard_map/gather/pallas_call | solution.py:356
  86.2 3.7 %modes.1 = (bf16[16,3,8,2048]{3,2,1,0:T(8,128)(2,1)}, f32[8,1,8]{2,1,0:T(1,128)}) custom-call(bf16[3,256,2048]{2,1,0:T(8,128)(2,1)S(1)} %get-tuple-element.7.coef, f32[2,16,128]{2,1,0:T(8,128)S(1)} %get-tuple-element.8.gram_ref, f32[1,2048]{1,0:T(1,128)S(1)} %get-tuple-element.9.weight), custom_call_target="tpu_custom_call" | custom-call | tf_op jit(solution)/shard_map/modes/pallas_call | solution.py:394

commit v6 on v4

--- a/solution.py
+++ b/solution.py
@@ -23,9 +23,12 @@
 TMS = 2
 SPACE = 4
 BLK = 8
+HALF = BLK // 2
 BLOCKS = TMS * BLK
 FIELDS = 3
 TREC = 296
+SECOND = HALF * NFFT // 2
+SPAN = TREC - SECOND
 CELLS = 2048
 NSLAB = 16
 SLOTS = TMS * SECTORS
@@ -56,19 +59,18 @@
 
 def spread_time_table():
     basis = time_table().astype(np.float32)
-    wide = np.zeros((NFREQ, BLK, 2, BLK, NFFT), np.float32)
-    for b in range(BLK):
+    wide = np.zeros((NFREQ, HALF, 2, HALF, NFFT), np.float32)
+    for b in range(HALF):
         wide[:, b, :, b, :] = basis.transpose(1, 0, 2)
-    return wide.reshape(NFREQ * ROWS, BLK * NFFT).astype(ml_dtypes.bfloat16)
+    return wide.reshape(NFREQ * 2 * HALF, HALF * NFFT).astype(ml_dtypes.bfloat16)
 
 
 def spread_order_table():
     table = order_table().astype(np.float32)
-    wide = np.zeros((2, ORDERS, TMS, BLK, TMS, SECTORS, BLK, 2), np.float32)
-    for j in range(TMS):
-        for b in range(BLK):
-            wide[:, :, j, b, j, :, b, :] = table.transpose(1, 0, 2, 3)
-    return wide.reshape(2 * ORDERS * BLOCKS, SLOTS * ROWS).astype(ml_dtypes.bfloat16)
+    wide = np.zeros((2, ORDERS, BLK, SECTORS, BLK, 2), np.float32)
+    for b in range(BLK):
+        wide[:, :, b, :, b, :] = table.transpose(1, 0, 2, 3)
+    return wide.reshape(2 * ORDERS * BLK, SECTORS * ROWS).astype(ml_dtypes.bfloat16)
 
 
 def place():
@@ -141,22 +143,29 @@
     for load in (smalls[0], smalls[1], loads[0], *loads[1:], *smalls[2:]):
         load.start()
     smalls[0].wait()
-    step = lax.broadcasted_iota(jnp.int32, (NFFT, TREC), 1) - lax.broadcasted_iota(
-        jnp.int32, (NFFT, TREC), 0
+    step = lax.broadcasted_iota(jnp.int32, (NFFT, SPAN), 1) - lax.broadcasted_iota(
+        jnp.int32, (NFFT, SPAN), 0
     )
-    for b in range(BLK):
-        shift[b * NFFT : (b + 1) * NFFT, :] = jnp.where(
-            step == start[tm * BLK + b], 1.0, 0.0
-        ).astype(BF)
+    for h in range(2):
+        for b in range(HALF):
+            shift[h, b * NFFT : (b + 1) * NFFT, :] = jnp.where(
+                step == start[tm * BLK + h * HALF + b] - h * SECOND, 1.0, 0.0
+            ).astype(BF)
     smalls[1].wait()
-    band[...] = jnp.dot(basis[...], shift[...], preferred_element_type=F32).astype(BF)
+    for h in range(2):
+        band[h] = jnp.dot(basis[...], shift[h], preferred_element_type=F32).astype(BF)
 
     copies, owns = [], []
     for n, (k, first, size) in enumerate(CHUNKS):
         loads[n].wait()
         span = pl.ds(first, size)
-        out = jnp.dot(band[...], rec[k, :, span], preferred_element_type=F32)
-        send[k, :, :, span] = out.astype(BF).reshape(NFREQ, ROWS, size)
+        halves = [
+            jnp.dot(
+                band[h], rec[k, h * SECOND : h * SECOND + SPAN, span], preferred_element_type=F32
+            ).reshape(NFREQ, 2 * HALF, size)
+            for h in range(2)
+        ]
+        send[k, :, :, span] = jnp.concatenate(halves, 1).astype(BF)
 
         if n == 0:
             pl.semaphore_wait(barrier, len(ORDER) + SPACE - 1)
@@ -189,8 +198,15 @@
             copy.wait_recv()
         owns[n].wait()
         span = pl.ds(first, size)
-        arrived = recv[k, :, :, span].reshape(SLOTS * ROWS, size)
-        c = jnp.dot(mixer[...], arrived, preferred_element_type=F32).astype(BF)
+        halves = [
+            jnp.dot(
+                mixer[...],
+                recv[k, j * SECTORS : (j + 1) * SECTORS, :, span].reshape(SECTORS * ROWS, size),
+                preferred_element_type=F32,
+            ).reshape(2 * ORDERS, BLK, size)
+            for j in range(TMS)
+        ]
+        c = jnp.concatenate(halves, 1).reshape(2 * ORDERS * BLOCKS, size).astype(BF)
         coef[k, :, span] = c
         weighted = (c.astype(F32) * weight[:, span]).astype(BF)
         acc[...] += lax.dot_general(
@@ -365,8 +381,8 @@
             pltpu.VMEM((1, CELLS), jnp.int32),
             pltpu.VMEM(basis.shape, BF),
             pltpu.VMEM(mixer.shape, BF),
-            pltpu.VMEM((NFREQ * ROWS, TREC), BF),
-            pltpu.VMEM((BLK * NFFT, TREC), BF),
+            pltpu.VMEM((2, NFREQ * 2 * HALF, SPAN), BF),
+            pltpu.VMEM((2, HALF * NFFT, SPAN), BF),
             pltpu.VMEM((width, width), F32),
             pltpu.VMEM((SPACE, 2, BLOCKS, LANES), F32),
             dma((5,)),

time: 89.1 us -> 89 us (level)
  no operation moved by 1% of the time
where the time goes in v6:
time: 89 us; the launch traced here: 88.8 us
  Pallas kernels  88.2 us (99%)
    pallas_call x1, Pallas kernels, local(): pl.pallas_call(gather_kernel, name='gather', out_shape=(jax.ShapeDtypeStr...  84.5 us
    pallas_call x1, Pallas kernels, local(): pl.pallas_call(modes_kernel, name='modes', out_shape=(jax.ShapeDtypeStruc...  3.69 us

profile of v6, /device:TPU:1, one launch (start us, length us, event | category | flops | bytes accessed | tf_op | source)
XLA Modules:
  0.0 88.8 jit_solution(3830287840107606238)
XLA Ops:
  0.6 84.5 %gather.1 = (bf16[3,256,2048]{2,1,0:T(8,128)(2,1)S(1)}, f32[2,16,128]{2,1,0:T(8,128)S(1)}, f32[1,2048]{1,0:T(1,128)S(1)}) custom-call(bf16[3,296,2048]{2,1,0:T(8,128)(2,1)} %bitcast.9, s32[16]{0:T(128)} %start_hbm.1, f32[16]{0:T(128)} %table_hbm.1, s32[1,2048]{1,0:T(1,128)} %bitcast.10, bf16[256,256]{1,0:T(8,128)(2,1)} %constant.4.clone.basis_hbm, ...), custom_call_target="tpu_custom_call" | custom-call | tf_op jit(solution)/shard_map/gather/pallas_call | solution.py:365
  85.2 3.7 %modes.1 = (bf16[16,3,8,2048]{3,2,1,0:T(8,128)(2,1)}, f32[8,1,8]{2,1,0:T(1,128)}) custom-call(bf16[3,256,2048]{2,1,0:T(8,128)(2,1)S(1)} %get-tuple-element.7.coef, f32[2,16,128]{2,1,0:T(8,128)S(1)} %get-tuple-element.8.gram_ref, f32[1,2048]{1,0:T(1,128)S(1)} %get-tuple-element.9.weight), custom_call_target="tpu_custom_call" | custom-call | tf_op jit(solution)/shard_map/modes/pallas_call | solution.py:403
